TPU v7x, 32 devices: a whole 2x2x4 slice. The times are simulated.
32 devices in a mesh: groups: 2 (over y), depth: 4 (over z), heads: 2 (over x), dp: 2 (over core).
Axes of the slice: x: 2, y: 2, z: 4, core: 2. Of those that a mesh axis runs over, the one named last changes fastest.
Arguments:
- queries: bfloat16 [4, 4096, 2560], P('depth', ('groups', 'dp'), 'heads'), parts along dimension 1, may hold values from -8 to 8
- grad_out: bfloat16 [4, 4096, 2560], P('depth', ('groups', 'dp'), 'heads'), parts along dimension 1, may hold values from -6 to 6
- key_rows: bfloat16 [4096, 512], P(('groups', 'depth', 'dp'), 'heads'), parts along dimension 0, may hold values from -4 to 4
- value_rows: bfloat16 [4096, 512], P(('groups', 'depth', 'dp'), 'heads'), parts along dimension 0, may hold values from -6 to 6
- doc_starts: int32 [32], P('groups'), parts along dimension 0, may hold values from 0 to 15, as said below
Outputs:
- attn_out: bfloat16 [4, 4096, 2560], P('depth', ('groups', 'dp'), 'heads'), parts along dimension 1
- grad_queries: bfloat16 [4, 4096, 2560], P('depth', ('groups', 'dp'), 'heads'), parts along dimension 1
- grad_keys: float32 [4096, 512], P(('groups', 'depth', 'dp'), 'heads'), parts along dimension 0
- grad_values: float32 [4096, 512], P(('groups', 'depth', 'dp'), 'heads'), parts along dimension 0
There are 2 independent parts, one for each index of `groups`. A program takes and returns all parts, laid end to end along the dimension named above; each array names one. Nothing has to cross between parts.
Inputs may be any that keep to these rules, and one draw needn't show every extreme that they name: doc_starts never falls, doc_starts[b] <= b, doc_starts[0] = 0, and the last block begins a document of its own.
All inputs are finite; a program needn't handle non-finite values.
Results may differ from a plain program's by a relative error of at most 0.02.
Values may be sent and summed in bfloat16 or wider, within the bound.
No kernel may reach another device: no remote copies, remote signals or barrier semaphores. Data moves between devices by JAX's collectives and lax.ppermute only.
A program may use at most 128 MiB of HBM per device.

v0:
```python
import jax
import jax.numpy as jnp
from jax import lax
from jax.sharding import PartitionSpec as P

HEAD_DIM = 128
QB = 128
GROUP = 5


NEG_FILL = -1e30


def allowed_pairs(query_pos, first_key, offset, key_count):
    key_pos = offset + jnp.arange(key_count, dtype=jnp.int32)
    return (key_pos[None, :] <= query_pos[:, None]) & (key_pos[None, :] >= first_key[:, None])


def online_step(running, key_piece, value_piece, offset, query_heads, query_pos, first_key):
    run_max, run_sum, accumulated = running
    key_count = key_piece.shape[0]
    key_heads = key_piece.reshape(key_count, -1, HEAD_DIM)
    value_heads = value_piece.reshape(key_count, -1, HEAD_DIM)
    scores = jnp.einsum(
        "kgrd,jkd->kgrj", query_heads, key_heads, preferred_element_type=jnp.float32
    ) * HEAD_DIM ** (-0.5)
    allowed = allowed_pairs(query_pos, first_key, offset, key_count)[None, None]
    scores = jnp.where(allowed, scores, NEG_FILL)
    new_max = jnp.maximum(run_max, jnp.max(scores, axis=-1))
    weights = jnp.where(allowed, jnp.exp(scores - new_max[..., None]), 0.0)
    factor = jnp.exp(run_max - new_max)
    run_sum = run_sum * factor + jnp.sum(weights, axis=-1)
    accumulated = accumulated * factor[..., None] + jnp.einsum(
        "kgrj,jkd->kgrd",
        weights.astype(jnp.bfloat16),
        value_heads,
        preferred_element_type=jnp.float32,
    )
    return (new_max, run_sum, accumulated)


def backward_step(
    query_grad_sum,
    key_piece,
    value_piece,
    offset,
    query_heads,
    grad_heads,
    row_dots,
    log_total,
    query_pos,
    first_key,
):
    key_count = key_piece.shape[0]
    softmax_scale = HEAD_DIM ** (-0.5)
    key_heads = key_piece.reshape(key_count, -1, HEAD_DIM)
    value_heads = value_piece.reshape(key_count, -1, HEAD_DIM)
    scores = (
        jnp.einsum("kgrd,jkd->kgrj", query_heads, key_heads, preferred_element_type=jnp.float32)
        * softmax_scale
    )
    allowed = allowed_pairs(query_pos, first_key, offset, key_count)[None, None]
    probabilities = jnp.where(
        allowed, jnp.exp(jnp.where(allowed, scores, NEG_FILL) - log_total[..., None]), 0.0
    )
    probs_low = probabilities.astype(jnp.bfloat16)
    value_grad = jnp.einsum(
        "kgrj,kgrd->jkd", probs_low, grad_heads, preferred_element_type=jnp.float32
    )
    prob_grads = jnp.einsum(
        "kgrd,jkd->kgrj", grad_heads, value_heads, preferred_element_type=jnp.float32
    )
    score_grads = (probabilities * (prob_grads - row_dots[..., None]) * softmax_scale).astype(
        jnp.bfloat16
    )
    query_grad_sum = query_grad_sum + jnp.einsum(
        "kgrj,jkd->kgrd", score_grads, key_heads, preferred_element_type=jnp.float32
    )
    key_grad = jnp.einsum(
        "kgrj,kgrd->jkd", score_grads, query_heads, preferred_element_type=jnp.float32
    )
    return (query_grad_sum, key_grad.reshape(key_count, -1), value_grad.reshape(key_count, -1))


def per_device(queries, grad_out, key_rows, value_rows, doc_starts):
    row_count = queries.shape[1]
    query_width = queries.shape[2]
    kv_count = key_rows.shape[1] // HEAD_DIM
    kv_width = key_rows.shape[1]
    depth_count = lax.axis_size("depth")
    core_count = lax.axis_size("dp")
    shard_rows = key_rows.shape[0]
    seq_len = shard_rows * depth_count * core_count
    block_len = min(256, seq_len)
    block_count = seq_len // block_len
    tile_len = min(256, row_count)
    tile_count = row_count // tile_len
    query_pos = lax.axis_index("dp") * row_count + jnp.arange(row_count, dtype=jnp.int32)
    block_ids = jnp.arange(doc_starts.shape[0], dtype=jnp.int32)
    first_key = (
        jnp.sum(
            jnp.where((query_pos // QB)[:, None] == block_ids[None, :], doc_starts[None, :], 0),
            axis=1,
        )
        * QB
    )
    query_all = jnp.transpose(
        queries[0].reshape(row_count, kv_count, GROUP, HEAD_DIM), (1, 2, 0, 3)
    )
    grad_all = jnp.transpose(
        grad_out[0].reshape(row_count, kv_count, GROUP, HEAD_DIM), (1, 2, 0, 3)
    )
    tile_query = []
    tile_grad = []
    tile_pos = []
    tile_first = []
    tile_low = []
    tile_last = []
    for tile in range(tile_count):
        lower = tile * tile_len
        upper = lower + tile_len
        tile_query.append(query_all[:, :, lower:upper])
        tile_grad.append(grad_all[:, :, lower:upper])
        tile_pos.append(query_pos[lower:upper])
        tile_first.append(first_key[lower:upper])
        tile_low.append(jnp.min(first_key[lower:upper]))
        tile_last.append(query_pos[upper - 1])
    key_full, value_full = (
        lax.all_gather(key_rows, ("depth", "dp"), axis=0, tiled=True),
        lax.all_gather(value_rows, ("depth", "dp"), axis=0, tiled=True),
    )
    key_blocks = key_full.reshape(block_count, block_len, kv_width)
    value_blocks = value_full.reshape(block_count, block_len, kv_width)
    states = []
    for tile in range(tile_count):

        def forward_block(index, running, which=tile):
            return online_step(
                running,
                key_blocks[index],
                value_blocks[index],
                index * block_len,
                tile_query[which],
                tile_pos[which],
                tile_first[which],
            )

        states.append(
            lax.fori_loop(
                tile_low[tile] // block_len,
                tile_last[tile] // block_len + 1,
                forward_block,
                (
                    jnp.full((kv_count, GROUP, tile_len), NEG_FILL, jnp.float32),
                    jnp.zeros((kv_count, GROUP, tile_len), jnp.float32),
                    jnp.zeros((kv_count, GROUP, tile_len, HEAD_DIM), jnp.float32),
                ),
            )
        )
    empty_store = jnp.zeros((block_count, block_len, kv_width), jnp.float32)
    key_terms = empty_store
    value_terms = empty_store
    attention_tiles = []
    query_grad_tiles = []
    for tile in range(tile_count):
        run_max, run_sum, accumulated = states[tile]
        log_total = run_max + jnp.log(run_sum)
        attention = (accumulated / run_sum[..., None]).astype(jnp.bfloat16)
        row_dots = jnp.sum(
            tile_grad[tile].astype(jnp.float32) * attention.astype(jnp.float32), axis=-1
        )

        def backward_block(index, carried, which=tile, dots=row_dots, totals=log_total):
            query_grad_sum, key_store, value_store = carried
            query_grad_sum, key_grad, value_grad = backward_step(
                query_grad_sum,
                key_blocks[index],
                value_blocks[index],
                index * block_len,
                tile_query[which],
                tile_grad[which],
                dots,
                totals,
                tile_pos[which],
                tile_first[which],
            )
            return (
                query_grad_sum,
                key_store.at[index].add(key_grad),
                value_store.at[index].add(value_grad),
            )

        query_grad_sum, key_terms, value_terms = lax.fori_loop(
            tile_low[tile] // block_len,
            tile_last[tile] // block_len + 1,
            backward_block,
            (jnp.zeros((kv_count, GROUP, tile_len, HEAD_DIM), jnp.float32), key_terms, value_terms),
        )
        attention_tiles.append(attention)
        query_grad_tiles.append(query_grad_sum.astype(jnp.bfloat16))
    key_term = key_terms.reshape(seq_len, -1)
    value_term = value_terms.reshape(seq_len, -1)
    key_grad, value_grad = (
        lax.psum_scatter(
            key_term.astype(jnp.bfloat16), ("depth", "dp"), scatter_dimension=0, tiled=True
        ).astype(jnp.float32),
        lax.psum_scatter(
            value_term.astype(jnp.bfloat16), ("depth", "dp"), scatter_dimension=0, tiled=True
        ).astype(jnp.float32),
    )
    attention_all = jnp.transpose(jnp.concatenate(attention_tiles, axis=2), (2, 0, 1, 3))
    query_grad = jnp.transpose(jnp.concatenate(query_grad_tiles, axis=2), (2, 0, 1, 3))
    return (
        attention_all.reshape(1, row_count, query_width),
        query_grad.reshape(1, row_count, query_width),
        key_grad,
        value_grad,
    )


def solution(mesh):
    in_specs = (
        P("depth", ("groups", "dp"), "heads"),
        P("depth", ("groups", "dp"), "heads"),
        P(("groups", "depth", "dp"), "heads"),
        P(("groups", "depth", "dp"), "heads"),
        P("groups"),
    )
    out_specs = (
        P("depth", ("groups", "dp"), "heads"),
        P("depth", ("groups", "dp"), "heads"),
        P(("groups", "depth", "dp"), "heads"),
        P(("groups", "depth", "dp"), "heads"),
    )
    return jax.shard_map(
        per_device, mesh=mesh, in_specs=in_specs, out_specs=out_specs, check_vma=False
    )
```

profile of v0, /device:TPU:0, one launch (start us, length us, event | category | flops | bytes accessed | tf_op | source)
XLA Modules:
  0.0 388.3 jit_solution(8086050353042929292)
XLA Ops:
  32.4 4.5 %copy.248 = bf16[1,1024,1280]{1,2,0:T(8,128)(2,1)} copy(bf16[1,1024,1280]{2,1,0:T(8,128)(2,1)} %param.38) | data formatting | bytes 5242880 | tf_op args[1]
  39.6 4.4 %fusion.107 = (bf16[2,5,256,128]{2,3,1,0:T(8,128)(2,1)}, bf16[2,5,256,128]{2,3,1,0:T(8,128)(2,1)}, bf16[2,5,256,128]{2,3,1,0:T(8,128)(2,1)}, bf16[2,5,256,128]{2...) fusion(bf16[2,5,1024,128]{2,3,1,0:T(8,128)(2,1)} %bitcast.536, ...), kind=kLoop, calls=%fused_computation.202 | loop fusion | bytes 10485760 | tf_op jit(solution)/shard_map/slice | solution.py:123
  50.5 7.2 %all-gather.5.cloned.1.call-done = bf16[2048,256]{1,0:T(8,128)(2,1)} async-done(((bf16[256,256]{1,0:T(8,128)(2,1)}), bf16[2048,256]{1,0:T(8,128)(2,1)}) %all-gather.5.cloned.1.call-update) | async-done | bytes 1048592 | tf_op jit(solution)/shard_map/all_gather | solution.py:130
  61.0 13.9 %while.121 = (s32[]{:T(128)}, f32[2,5,256]{2,1,0:T(8,128)S(1)}, f32[2,5,256]{2,1,0:T(8,128)}, f32[2,5,256,128]{3,2,1,0:T(8,128)}, s32[]{:T(128)}, /*index=5*/s32...) while((s32[]{:T(128)}, f32[2,5,256]{2,1,0:T(8,128)S(1)}, ...), condition=%wide.region_10.11_spmd, body=%wide.region_7.10_spmd.sunk | while | flops 344921344 | bytes 23449928 | solution.py:149
  75.0 2.8 copy.239
  80.1 15.0 %while.122 = (s32[]{:T(128)}, f32[2,5,256]{2,1,0:T(8,128)}, f32[2,5,256]{2,1,0:T(8,128)}, f32[2,5,256,128]{3,2,1,0:T(8,128)}, s32[]{:T(128)}, /*index=5*/s32[256...) while((s32[]{:T(128)}, f32[2,5,256]{2,1,0:T(8,128)}, ...), condition=%wide.region_15.16_spmd, body=%wide.region_12.15_spmd.sunk | while | flops 344921344 | bytes 23490916 | solution.py:149
  95.1 2.8 copy.243
  99.7 6.9 %while.123 = (s32[]{:T(128)}, f32[2,5,256]{2,1,0:T(8,128)S(1)}, f32[2,5,256]{2,1,0:T(8,128)}, f32[2,5,256,128]{3,2,1,0:T(8,128)}, s32[]{:T(128)}, /*index=5*/s32...) while((s32[]{:T(128)}, f32[2,5,256]{2,1,0:T(8,128)S(1)}, ...), condition=%wide.region_20.21_spmd, body=%wide.region_17.20_spmd.sunk | while | flops 344921344 | bytes 23449928 | solution.py:149
  106.6 2.8 copy.247
  111.2 6.9 %while.120 = (s32[]{:T(128)}, f32[2,5,256]{2,1,0:T(8,128)S(1)}, f32[2,5,256]{2,1,0:T(8,128)}, f32[2,5,256,128]{3,2,1,0:T(8,128)}, s32[]{:T(128)}, /*index=5*/s32...) while((s32[]{:T(128)}, f32[2,5,256]{2,1,0:T(8,128)S(1)}, ...), condition=%wide.region_5.6_spmd, body=%wide.region_2.5_spmd.sunk | while | flops 344921344 | bytes 23449928 | solution.py:149
  118.2 3.6 copy.235
  122.5 6.5 %multiply_reduce_fusion = (f32[2,5,256]{2,1,0:T(8,128)}, f32[2,5,256]{2,1,0:T(8,128)S(1)}, f32[2,5,256]{2,1,0:T(8,128)S(1)}, f32[2,5,256]{2,1,0:T(8,128)S(1)}, b...) fusion(bf16[2,5,1024,128]{2,3,1,0:T(8,128)(2,1)} %bitcast.537, ...), kind=kLoop, calls=%fused_computation.174 | loop fusion | flops 7854080 | bytes 10567680 | tf_op jit(solution)/shard_map/reduce_sum | solution.py:169
  132.2 12.8 %while.124 = (s32[]{:T(128)}, f32[2,5,256,128]{3,2,1,0:T(8,128)S(1)}, f32[8,256,256]{1,2,0:T(8,128)}, f32[8,256,256]{1,2,0:T(8,128)}, s32[]{:T(128)}, /*index=5*...) while((s32[]{:T(128)}, ...), condition=%wide.region_24.25_spmd, body=%wide.region_22.24_spmd.sunk | while | flops 848167168 | bytes 33393972 | solution.py:193
  136.3 3.2 fusion.286
  146.6 27.5 %while.125 = (s32[]{:T(128)}, f32[2,5,256,128]{3,2,1,0:T(8,128)}, f32[8,256,256]{1,2,0:T(8,128)}, f32[8,256,256]{1,2,0:T(8,128)}, s32[]{:T(128)}, /*index=5*/s32...) while((s32[]{:T(128)}, f32[2,5,256,128]{3,2,1,0:T(8,128)}, ...), condition=%wide.region_28.29_spmd, body=%wide.region_26.28_spmd.sunk | while | flops 848167168 | bytes 43879788 | solution.py:193
  150.7 3.0 fusion.301
  164.4 3.0 fusion.301
  174.3 25.8 %while.126 = (s32[]{:T(128)}, f32[2,5,256,128]{3,2,1,0:T(8,128)S(1)}, f32[8,256,256]{1,2,0:T(8,128)}, f32[8,256,256]{1,2,0:T(8,128)}, s32[]{:T(128)}, /*index=5*...) while((s32[]{:T(128)}, ...), condition=%wide.region_32.33_spmd, body=%wide.region_30.32_spmd.sunk | while | flops 848167168 | bytes 33393972 | solution.py:193
  178.6 3.2 fusion.316
  191.3 3.2 fusion.316
  202.0 12.6 %while.127 = (s32[]{:T(128)}, f32[2,5,256,128]{3,2,1,0:T(8,128)}, f32[8,256,256]{1,2,0:T(8,128)}, f32[8,256,256]{1,2,0:T(8,128)}, s32[]{:T(128)}, /*index=5*/s32...) while((s32[]{:T(128)}, f32[2,5,256,128]{3,2,1,0:T(8,128)}, ...), condition=%wide.region_36.37_spmd, body=%wide.region_34.36_spmd.sunk | while | flops 848167168 | bytes 22949172 | solution.py:193
  211.6 3.0 convolution_add_fusion.23
  235.8 111.6 %reduce-scatter.3.cloned.1.call-done = bf16[256,256]{1,0:T(8,128)(2,1)} async-done(((bf16[2048,256]{1,0:T(8,128)(2,1)}), bf16[256,256]{1,0:T(8,128)(2,1)}) %reduce-scatter.3.cloned.1.call-update) | async-done | bytes 131088 | tf_op jit(solution)/shard_map/reduce_scatter | solution.py:204
  349.0 31.1 %reduce-scatter.5.cloned.1.call-done = bf16[256,256]{1,0:T(8,128)(2,1)} async-done(((bf16[2048,256]{1,0:T(8,128)(2,1)}), bf16[256,256]{1,0:T(8,128)(2,1)}) %reduce-scatter.5.cloned.1.call-update) | async-done | bytes 131088 | tf_op jit(solution)/shard_map/reduce_scatter | solution.py:207
  (330 shorter events, 155.8 us)
Async XLA Ops:
  7.2 41.9 %all-gather.3.cloned.1.call-start = ((), (), s32[]{:S(2)}) async-start(), calls=%async_computation.2 | async-start | bytes 1179648 | tf_op jit(solution)/shard_map/all_gather | solution.py:129
  7.9 49.9 %all-gather.5.cloned.1.call-start = ((), (), s32[]{:S(2)}) async-start(), calls=%async_computation.3 | async-start | bytes 1179648 | tf_op jit(solution)/shard_map/all_gather | solution.py:130
  8.6 338.8 %reduce-scatter.3.cloned.1.call-start = ((), (), s32[]{:S(2)}) async-start(), calls=%async_computation.4 | async-start | bytes 1179648 | tf_op jit(solution)/shard_map/reduce_scatter | solution.py:204
  32.4 4.6 %copy-start.27 = (bf16[1,1024,1280]{2,1,0:T(8,128)(2,1)S(1)}, bf16[1,1024,1280]{2,1,0:T(8,128)(2,1)}, u32[]{:S(2)}) copy-start(bf16[1,1024,1280]{2,1,0:T(8,128)(2,1)} %param.37) | copy-start | bytes 7864324
  43.9 4.5 %copy-start = (bf16[2,5,256,128]{2,3,1,0:T(8,128)(2,1)}, bf16[2,5,256,128]{2,3,1,0:T(8,128)(2,1)S(1)}, u32[]{:S(2)}) copy-start(bf16[2,5,256,128]{2,3,1,0:T(8,128)(2,1)S(1)} %get-tuple-element.2133) | copy-start | bytes 1966084
  43.9 4.5 %copy-start.2 = (bf16[2,5,256,128]{2,3,1,0:T(8,128)(2,1)}, bf16[2,5,256,128]{2,3,1,0:T(8,128)(2,1)S(1)}, u32[]{:S(2)}) copy-start(bf16[2,5,256,128]{2,3,1,0:T(8,128)(2,1)S(1)} %get-tuple-element.2076) | copy-start | bytes 1966084
  74.9 5.2 %copy-start.29 = (f32[2,5,256]{2,1,0:T(8,128)}, f32[2,5,256]{2,1,0:T(8,128)S(1)}, u32[]{:S(2)}) copy-start(f32[2,5,256]{2,1,0:T(8,128)S(1)} %get-tuple-element.612) | copy-start | bytes 30724
  118.2 10.8 %copy-start.13 = (bf16[8,256,256]{1,2,0:T(8,128)(2,1)}, bf16[8,256,256]{1,2,0:T(8,128)(2,1)S(1)}, u32[]{:S(2)}) copy-start(bf16[8,256,256]{1,2,0:T(8,128)(2,1)S(1)} %get-tuple-element.2189) | copy-start | bytes 3145732
  118.2 10.8 %copy-start.14 = (bf16[8,256,256]{1,2,0:T(8,128)(2,1)}, bf16[8,256,256]{1,2,0:T(8,128)(2,1)S(1)}, u32[]{:S(2)}) copy-start(bf16[8,256,256]{1,2,0:T(8,128)(2,1)S(1)} %get-tuple-element.2196) | copy-start | bytes 3145732
  118.2 4.3 %copy-start.37 = (f32[2,5,256]{2,1,0:T(8,128)S(1)}, f32[2,5,256]{2,1,0:T(8,128)}, u32[]{:S(2)}) copy-start(f32[2,5,256]{2,1,0:T(8,128)} %get-tuple-element.603) | copy-start | bytes 30724
  118.2 4.3 %copy-start.40 = (f32[2,5,256]{2,1,0:T(8,128)S(1)}, f32[2,5,256]{2,1,0:T(8,128)}, u32[]{:S(2)}) copy-start(f32[2,5,256]{2,1,0:T(8,128)} %get-tuple-element.605) | copy-start | bytes 30724
  132.2 12.8 %copy-start.30 = (f32[2,5,256]{2,1,0:T(8,128)S(1)}, f32[2,5,256]{2,1,0:T(8,128)}, u32[]{:S(2)}) copy-start(f32[2,5,256]{2,1,0:T(8,128)} %copy-done.29) | copy-start | bytes 30724
  132.2 14.2 %copy-start.54 = (s32[256]{0:T(256)S(1)}, s32[256]{0:T(256)}, u32[]{:S(2)}) copy-start(s32[256]{0:T(256)} %get-tuple-element.2217) | copy-start | bytes 3076
  132.2 14.2 %copy-start.58 = (s32[256]{0:T(256)S(1)}, s32[256]{0:T(256)}, u32[]{:S(2)}) copy-start(s32[256]{0:T(256)} %get-tuple-element.2221) | copy-start | bytes 3076
  146.4 27.7 %copy-start.32 = (f32[2,5,256]{2,1,0:T(8,128)S(1)}, f32[2,5,256]{2,1,0:T(8,128)}, u32[]{:S(2)}) copy-start(f32[2,5,256]{2,1,0:T(8,128)} %get-tuple-element.616) | copy-start | bytes 30724
  146.4 27.8 %copy-start.3 = (bf16[2,5,256,128]{2,3,1,0:T(8,128)(2,1)S(1)}, bf16[2,5,256,128]{2,3,1,0:T(8,128)(2,1)}, u32[]{:S(2)}) copy-start(bf16[2,5,256,128]{2,3,1,0:T(8,128)(2,1)} %copy-done.2) | copy-start | bytes 1966084
  146.4 27.8 %copy-start.53 = (s32[256]{0:T(256)S(1)}, s32[256]{0:T(256)}, u32[]{:S(2)}) copy-start(s32[256]{0:T(256)} %get-tuple-element.2216) | copy-start | bytes 3076
  146.5 27.8 %copy-start.57 = (s32[256]{0:T(256)S(1)}, s32[256]{0:T(256)}, u32[]{:S(2)}) copy-start(s32[256]{0:T(256)} %get-tuple-element.2220) | copy-start | bytes 3076
  174.2 25.9 %copy-start.34 = (f32[2,5,256]{2,1,0:T(8,128)S(1)}, f32[2,5,256]{2,1,0:T(8,128)}, u32[]{:S(2)}) copy-start(f32[2,5,256]{2,1,0:T(8,128)} %copy-done.33) | copy-start | bytes 30724
  174.3 27.7 %copy-start.1 = (bf16[2,5,256,128]{2,3,1,0:T(8,128)(2,1)S(1)}, bf16[2,5,256,128]{2,3,1,0:T(8,128)(2,1)}, u32[]{:S(2)}) copy-start(bf16[2,5,256,128]{2,3,1,0:T(8,128)(2,1)} %copy-done) | copy-start | bytes 1966084
  174.3 27.7 %copy-start.52 = (s32[256]{0:T(256)S(1)}, s32[256]{0:T(256)}, u32[]{:S(2)}) copy-start(s32[256]{0:T(256)} %get-tuple-element.2215) | copy-start | bytes 3076
  174.3 27.7 %copy-start.56 = (s32[256]{0:T(256)S(1)}, s32[256]{0:T(256)}, u32[]{:S(2)}) copy-start(s32[256]{0:T(256)} %get-tuple-element.2219) | copy-start | bytes 3076
  217.7 162.5 %reduce-scatter.5.cloned.1.call-start = ((), (), s32[]{:S(2)}) async-start(), calls=%async_computation.5 | async-start | bytes 1179648 | tf_op jit(solution)/shard_map/reduce_scatter | solution.py:207
  220.8 5.2 %copy-start.8 = (f32[2,5,256,128]{3,2,1,0:T(8,128)S(1)}, f32[2,5,256,128]{3,2,1,0:T(8,128)}, u32[]{:S(2)}) copy-start(f32[2,5,256,128]{3,2,1,0:T(8,128)} %copy-done.7) | copy-start | bytes 3932164
  (59 other events, 155.7 us)
Sparse Core Ops, SparseCore 0:
  9.6 24.8 all-gather.2
  36.1 21.6 all-gather.4
  217.8 129.5 reduce-scatter.2
  349.5 30.5 reduce-scatter.4
where the time goes:
time: 381 us; the launch traced here: 388 us
  waiting for transfers between devices  151 us (40%)
  local copies, waits for them, and re-layouts  88.9 us (23%)
  matrix products  62.3 us (16%)
  other arithmetic  49 us (13%)
  between operations  35.1 us (9%)
    reduce_scatter x1, waiting for transfers between devices, per_device(): lax.psum_scatter(key_term.astype(jnp.bfloat16), ('depth', 'dp'), scatter_...  112 us
    reduce_scatter x1, waiting for transfers between devices, per_device(): lax.psum_scatter(value_term.astype(jnp.bfloat16), ('depth', 'dp'), scatte...  31.1 us
    while x14, local copies, waits for them, and re-layouts, per_device(): lax.fori_loop(tile_low[tile] // block_len, tile_last[tile] // block_len +...  25.8 us
    dot_general x6, matrix products, backward_step(): jnp.einsum('kgrd,jkd->kgrj', grad_heads, value_heads, preferred_element_t...  17.7 us
    scatter-add x6, other arithmetic, backward_block(): key_store.at[index].add(key_grad)  15.4 us
    while x102, local copies, waits for them, and re-layouts  13.4 us
    unnamed x66, local copies, waits for them, and re-layouts  12.8 us
    dot_general x6, matrix products, online_step(): jnp.einsum('kgrd,jkd->kgrj', query_heads, key_heads, preferred_element_ty...  10.9 us
  transfers between devices with their start and end apart: 4, of which 3 were waited for; matrix products, arithmetic and copies ran while one was open for 10% of the time, Pallas kernels for 0%

commit v1 on v0

v1 whole, which is shorter than its diff:
```python
import functools
import math

import jax
import jax.numpy as jnp
from jax import lax
from jax.experimental import pallas as pl
from jax.experimental.pallas import tpu as pltpu
from jax.sharding import PartitionSpec as P

HEAD_DIM = 128
QB = 128
GROUP = 5
GW = GROUP * HEAD_DIM
NEG_FILL = -1e30
SCALE = HEAD_DIM ** -0.5
SCALE2 = SCALE * math.log2(math.e)
NT = (((1,), (1,)), ((), ()))
TN = (((0,), (0,)), ((), ()))
VMEM_LIMIT = 56 * 1024 * 1024


def dot(left, right, dims=(((1,), (0,)), ((), ()))):
    return lax.dot_general(left, right, dims, preferred_element_type=jnp.float32)


def first_keys(docs, block, count, axis):
    lane = lax.broadcasted_iota(jnp.int32, (1, count * QB) if axis else (count * QB, 1), axis)
    first = jnp.zeros(lane.shape, jnp.int32)
    for part in range(count):
        first = jnp.where(lane >= part * QB, docs[block + part] * QB, first)
    return first, block * QB + lane


def bias_of(key_pos, query_pos, first, upper):
    allowed = (key_pos <= query_pos) & (key_pos >= first) & (key_pos < upper)
    return jnp.where(allowed, 0.0, NEG_FILL)


def stack_heads(block):
    return jnp.concatenate([block[:, g * HEAD_DIM:(g + 1) * HEAD_DIM] for g in range(GROUP)], axis=0)


def pick(step, local_blocks, refs):
    if len(refs) == 1:
        return refs[0][...]
    return jnp.where(step < local_blocks, refs[0][...], refs[1][...])


def query_block(meta, step, local_blocks, count):
    part = step // local_blocks
    return meta[1 + part] + (step - part * local_blocks) * count


def tile_start(end, tile, width):
    return pl.multiple_of(jnp.maximum((end - width * (tile + 1)) * QB, 0), QB)


def value_kernel(local_blocks, parts, count, width, meta, docs, *refs):
    queries, refs = refs[:parts], refs[parts:]
    grads, refs = refs[:parts], refs[parts:]
    key_ref, total_ref, out_ref, value_sum, score_store = refs
    step = pl.program_id(1)
    span = width * QB
    block = query_block(meta, step, local_blocks, count)
    end = block + count
    tiles = (end - docs[block] + width - 1) // width
    query = stack_heads(pick(step, local_blocks, queries))
    grad = stack_heads(pick(step, local_blocks, grads))
    first, query_pos = first_keys(docs, block, count, 1)

    @pl.when(step == 0)
    def _():
        value_sum[...] = jnp.zeros_like(value_sum)

    def scores_of(tile):
        start = tile_start(end, tile, width)
        key_pos = start + lax.broadcasted_iota(jnp.int32, (span, 1), 0)
        bias = bias_of(key_pos, query_pos, first, (end - width * tile) * QB)
        scores = dot(key_ref[pl.ds(start, span), :], query, NT) + jnp.concatenate([bias] * GROUP, axis=1)
        return scores

    scores = scores_of(0)
    score_store[0] = scores

    def score_tile(tile, best):
        scores = scores_of(tile)
        score_store[tile] = scores
        return jnp.maximum(best, jnp.max(scores, axis=0, keepdims=True))

    best = lax.fori_loop(1, tiles, score_tile, jnp.max(scores, axis=0, keepdims=True)) * SCALE2
    weights = jnp.exp2(scores * SCALE2 - best)
    score_store[0] = weights

    def weight_tile(tile, total):
        weights = jnp.exp2(score_store[tile] * SCALE2 - best)
        score_store[tile] = weights
        return total + jnp.sum(weights, axis=0, keepdims=True)

    total = lax.fori_loop(1, tiles, weight_tile, jnp.sum(weights, axis=0, keepdims=True))
    inverse = 1.0 / total
    total_ref[...] = (best + jnp.log2(total))[None, None]

    def value_tile(tile, carry):
        start = tile_start(end, tile, width)
        low = (score_store[tile] * inverse).astype(jnp.bfloat16)
        value_sum[pl.ds(start, span), :] += dot(low, grad)
        return carry

    value_tile(0, 0)
    lax.fori_loop(1, tiles, value_tile, 0)

    @pl.when(step == pl.num_programs(1) - 1)
    def _():
        out_ref[...] = value_sum[...].astype(out_ref.dtype)


def query_kernel(local_blocks, parts, count, width, meta, docs, *refs):
    queries, refs = refs[:parts], refs[parts:]
    grads, refs = refs[:parts], refs[parts:]
    key_ref, value_ref, total_ref = refs[:3]
    refs = refs[3:]
    attns, refs = refs[:parts], refs[parts:]
    query_grads, refs = refs[:parts], refs[parts:]
    key_out, key_sum, prob_store, attn_sum, grad_sum = refs
    step = pl.program_id(1)
    span = width * QB
    rows = count * QB
    block = query_block(meta, step, local_blocks, count)
    end = block + count
    tiles = (end - docs[block] + width - 1) // width
    query = stack_heads(pick(step, local_blocks, queries))
    grad = stack_heads(pick(step, local_blocks, grads))
    first, query_pos = first_keys(docs, block, count, 0)
    total = jnp.concatenate(
        [
            jnp.transpose(jnp.broadcast_to(total_ref[0, 0, :, g * QB:(g + 1) * QB], (8, QB)))[:, :1]
            for g in range(GROUP * count)
        ],
        axis=0,
    )

    @pl.when(step == 0)
    def _():
        key_sum[...] = jnp.zeros_like(key_sum)

    def weights_of(tile):
        start = tile_start(end, tile, width)
        key_pos = start + lax.broadcasted_iota(jnp.int32, (1, span), 1)
        bias = bias_of(key_pos, query_pos, first, (end - width * tile) * QB)
        scores = dot(query, key_ref[pl.ds(start, span), :], NT) + jnp.concatenate([bias] * GROUP, axis=0)
        weights = jnp.exp2(scores * SCALE2 - total)
        prob_store[tile] = weights
        return dot(weights.astype(jnp.bfloat16), value_ref[pl.ds(start, span), :])

    attn_sum[...] = weights_of(0)

    def attn_tile(tile, carry):
        attn_sum[...] += weights_of(tile)
        return carry

    lax.fori_loop(1, tiles, attn_tile, 0)
    attn = attn_sum[...].astype(jnp.bfloat16)
    row_dots = jnp.sum(grad.astype(jnp.float32) * attn.astype(jnp.float32), axis=1, keepdims=True)

    def grad_of(tile):
        start = tile_start(end, tile, width)
        keys = key_ref[pl.ds(start, span), :]
        prob_grads = dot(grad, value_ref[pl.ds(start, span), :], NT)
        score_grads = (prob_store[tile] * (prob_grads - row_dots)).astype(jnp.bfloat16)
        key_sum[pl.ds(start, span), :] += dot(score_grads, query, TN)
        return dot(score_grads, keys)

    grad_sum[...] = grad_of(0)

    def grad_tile(tile, carry):
        grad_sum[...] += grad_of(tile)
        return carry

    lax.fori_loop(1, tiles, grad_tile, 0)
    query_grad = (grad_sum[...] * SCALE).astype(jnp.bfloat16)

    def emit(attn_ref, grad_ref):
        for g in range(GROUP):
            attn_ref[:, g * HEAD_DIM:(g + 1) * HEAD_DIM] = attn[g * rows:(g + 1) * rows]
            grad_ref[:, g * HEAD_DIM:(g + 1) * HEAD_DIM] = query_grad[g * rows:(g + 1) * rows]

    for part in range(parts):
        if parts == 1:
            emit(attns[0], query_grads[0])
        else:
            pl.when(step // local_blocks == part)(functools.partial(emit, attns[part], query_grads[part]))

    @pl.when(step == pl.num_programs(1) - 1)
    def _():
        key_out[...] = (key_sum[...] * SCALE).astype(key_out.dtype)


def row_specs(local_blocks, parts, count):
    def own(head, step, meta, docs):
        return (jnp.minimum(step, local_blocks - 1), meta[0] + head)

    def received(head, step, meta, docs):
        return (jnp.maximum(step - local_blocks, 0), head)

    return [pl.BlockSpec((count * QB, GW), own), pl.BlockSpec((count * QB, GW), received)][:parts]


def kv_spec(seq_len):
    return pl.BlockSpec((seq_len, HEAD_DIM), lambda head, step, meta, docs: (0, head))


def total_spec(count):
    return pl.BlockSpec((1, 1, 1, count * GW), lambda head, step, meta, docs: (head, step, 0, 0))


def run_value(meta, docs, queries, grads, keys, count, width):
    parts = len(queries)
    local_blocks = queries[0].shape[0] // (count * QB)
    steps = local_blocks * parts
    seq_len = keys.shape[0]
    heads = keys.shape[1] // HEAD_DIM
    span = width * QB
    return pl.pallas_call(
        functools.partial(value_kernel, local_blocks, parts, count, width),
        grid_spec=pltpu.PrefetchScalarGridSpec(
            num_scalar_prefetch=2,
            grid=(heads, steps),
            in_specs=row_specs(local_blocks, parts, count) * 2 + [kv_spec(seq_len)],
            out_specs=[total_spec(count), kv_spec(seq_len)],
            scratch_shapes=[
                pltpu.VMEM((seq_len, HEAD_DIM), jnp.float32),
                pltpu.VMEM((pl.cdiv(seq_len, span), span, count * GW), jnp.float32),
            ],
        ),
        out_shape=[
            jax.ShapeDtypeStruct((heads, steps, 1, count * GW), jnp.float32),
            jax.ShapeDtypeStruct(keys.shape, jnp.bfloat16),
        ],
        compiler_params=pltpu.CompilerParams(vmem_limit_bytes=VMEM_LIMIT),
        name="value_grad",
    )(meta, docs, *queries, *grads, keys)


def run_query(meta, docs, queries, grads, keys, values, totals, count, width):
    parts = len(queries)
    local_blocks = queries[0].shape[0] // (count * QB)
    steps = local_blocks * parts
    seq_len = keys.shape[0]
    heads = keys.shape[1] // HEAD_DIM
    span = width * QB
    rows = row_specs(local_blocks, parts, count)
    shapes = [jax.ShapeDtypeStruct(q.shape, jnp.bfloat16) for q in queries]
    outs = pl.pallas_call(
        functools.partial(query_kernel, local_blocks, parts, count, width),
        grid_spec=pltpu.PrefetchScalarGridSpec(
            num_scalar_prefetch=2,
            grid=(heads, steps),
            in_specs=rows * 2 + [kv_spec(seq_len), kv_spec(seq_len), total_spec(count)],
            out_specs=rows * 2 + [kv_spec(seq_len)],
            scratch_shapes=[
                pltpu.VMEM((seq_len, HEAD_DIM), jnp.float32),
                pltpu.VMEM((pl.cdiv(seq_len, span), count * GW, span), jnp.float32),
                pltpu.VMEM((count * GW, HEAD_DIM), jnp.float32),
                pltpu.VMEM((count * GW, HEAD_DIM), jnp.float32),
            ],
        ),
        out_shape=shapes * 2 + [jax.ShapeDtypeStruct(keys.shape, jnp.bfloat16)],
        compiler_params=pltpu.CompilerParams(vmem_limit_bytes=VMEM_LIMIT),
        name="query_grad",
    )(meta, docs, *queries, *grads, keys, values, totals)
    return outs[:parts], outs[parts:2 * parts], outs[-1]


def shift_perm(depth_count, hops):
    return [(d, (d + hops) % depth_count) for d in range(depth_count)]


def gather_depth(rows, depth_count):
    me = lax.axis_index("depth")
    count = rows.shape[0]
    full = jnp.zeros((count * depth_count, rows.shape[1]), rows.dtype)
    pieces = [(0, rows)]
    for hops in range(1, depth_count):
        pieces.append((hops, lax.ppermute(rows, "depth", shift_perm(depth_count, hops))))
    for hops, piece in pieces:
        source = lax.rem(me - hops + depth_count, depth_count)
        full = lax.dynamic_update_slice(full, piece, (source * count, 0))
    return full


def head_columns(rows, which, width):
    return lax.dynamic_slice(rows, (0, which * width), (rows.shape[0], width))


def swap_cores(array):
    return lax.ppermute(array, "dp", [(0, 1), (1, 0)])


def spread_heads(rows, core, width):
    own = head_columns(rows, core, width)
    other = swap_cores(head_columns(rows, 1 - core, width))
    first = core == 0
    return jnp.concatenate([jnp.where(first, own, other), jnp.where(first, other, own)], axis=0)


def return_terms(terms, depth_count, core):
    me = lax.axis_index("depth")
    shard = terms.shape[0] // (2 * depth_count)
    sums = [[], []]
    for hops in range(depth_count):
        target = lax.rem(me + hops, depth_count)
        for flip in range(2):
            side = core if flip == 0 else 1 - core
            piece = lax.dynamic_slice(terms, ((2 * target + side) * shard, 0), (shard, terms.shape[1]))
            if hops or flip:
                perm = [
                    (2 * d + c, 2 * ((d + hops) % depth_count) + (c ^ flip))
                    for d in range(depth_count)
                    for c in range(2)
                ]
                piece = lax.ppermute(piece, ("depth", "dp"), perm)
            sums[flip].append(piece.astype(jnp.float32))
    own, other = sum(sums[0]), sum(sums[1])
    first = core == 0
    return jnp.concatenate([jnp.where(first, own, other), jnp.where(first, other, own)], axis=1)


def by_head(queries, grad_out, key_rows, value_rows, doc_starts):
    depth_count = lax.axis_size("depth")
    core = lax.axis_index("dp")
    local_blocks = queries.shape[0] // QB
    kv_width = key_rows.shape[1] // 2
    query_width = queries.shape[1] // 2
    heads = kv_width // HEAD_DIM
    keys = gather_depth(spread_heads(key_rows, core, kv_width), depth_count)
    values = gather_depth(spread_heads(value_rows, core, kv_width), depth_count)
    query_got = swap_cores(head_columns(queries, 1 - core, query_width))
    grad_got = swap_cores(head_columns(grad_out, 1 - core, query_width))
    meta = jnp.stack([core * heads, core * local_blocks, (1 - core) * local_blocks]).astype(jnp.int32)
    query_parts = [queries, query_got]
    grad_parts = [grad_out, grad_got]
    totals, value_terms = run_value(meta, doc_starts, query_parts, grad_parts, keys, 2, 3)
    attns, query_grads, key_terms = run_query(
        meta, doc_starts, query_parts, grad_parts, keys, values, totals, 2, 3
    )
    value_grad = return_terms(value_terms, depth_count, core)
    key_grad = return_terms(key_terms, depth_count, core)
    outs = []
    for own, send in (attns, query_grads):
        outs.append(lax.dynamic_update_slice(own, swap_cores(send), (0, (1 - core) * query_width)))
    return outs[0], outs[1], key_grad, value_grad


def by_rows(queries, grad_out, key_rows, value_rows, doc_starts):
    axes = ("depth", "dp")
    block = lax.axis_index("dp") * (queries.shape[0] // QB)
    keys = lax.all_gather(key_rows, axes, axis=0, tiled=True)
    values = lax.all_gather(value_rows, axes, axis=0, tiled=True)
    meta = jnp.stack([jnp.zeros_like(block), block]).astype(jnp.int32)
    totals, value_terms = run_value(meta, doc_starts, [queries], [grad_out], keys, 2, 3)
    attns, query_grads, key_terms = run_query(
        meta, doc_starts, [queries], [grad_out], keys, values, totals, 2, 3
    )
    value_grad = lax.psum_scatter(value_terms, axes, scatter_dimension=0, tiled=True)
    key_grad = lax.psum_scatter(key_terms, axes, scatter_dimension=0, tiled=True)
    return attns[0], query_grads[0], key_grad.astype(jnp.float32), value_grad.astype(jnp.float32)


def per_device(queries, grad_out, key_rows, value_rows, doc_starts):
    kv_count = key_rows.shape[1] // HEAD_DIM
    split = lax.axis_size("dp") == 2 and kv_count % 2 == 0
    body = by_head if split else by_rows
    attn, query_grad, key_grad, value_grad = body(
        queries[0], grad_out[0], key_rows, value_rows, doc_starts
    )
    return attn[None], query_grad[None], key_grad, value_grad


def solution(mesh):
    rows = P("depth", ("groups", "dp"), "heads")
    shared = P(("groups", "depth", "dp"), "heads")
    return jax.shard_map(
        per_device,
        mesh=mesh,
        in_specs=(rows, rows, shared, shared, P("groups")),
        out_specs=(rows, rows, shared, shared),
        check_vma=False,
    )
```

time: 381 us -> 123 us (0.32)
  the two profiles are of different devices: /device:TPU:0 before, /device:TPU:13 now
where the time goes in v1:
time: 123 us; the launch traced here: 122 us
  Pallas kernels  48.3 us (39%)
  waiting for transfers between devices  29.5 us (24%)
  starting transfers between devices  29.1 us (24%)
  local copies, waits for them, and re-layouts  10.7 us (9%)
  other arithmetic  3.53 us (3%)
    pallas_call x1, Pallas kernels, run_query(): pl.pallas_call(functools.partial(query_kernel, local_blocks, parts, count...  31 us
    ppermute x14, starting transfers between devices, return_terms(): piece = lax.ppermute(piece, ('depth', 'dp'), perm)  18.6 us
    pallas_call x1, Pallas kernels, run_value(): pl.pallas_call(functools.partial(value_kernel, local_blocks, parts, count...  17.3 us
    ppermute x6, waiting for transfers between devices, gather_depth(): lax.ppermute(rows, 'depth', shift_perm(depth_count, hops))  16.5 us
    ppermute x14, waiting for transfers between devices, return_terms(): piece = lax.ppermute(piece, ('depth', 'dp'), perm)  13.1 us
    ppermute x6, starting transfers between devices, gather_depth(): lax.ppermute(rows, 'depth', shift_perm(depth_count, hops))  8.38 us
    dynamic_slice x4, local copies, waits for them, and re-layouts, head_columns(): return lax.dynamic_slice(rows, (0, which * width), (rows.shape[0], width))  4.7 us
    unnamed x28, local copies, waits for them, and re-layouts  3.29 us
  transfers between devices with their start and end apart: 26, of which 12 were waited for; matrix products, arithmetic and copies ran while one was open for 8% of the time, Pallas kernels for 0%

profile of v1, /device:TPU:13, one launch (start us, length us, event | category | flops | bytes accessed | tf_op | source)
XLA Modules:
  0.0 122.1 jit_solution(14543692965018922485)
XLA Ops:
  2.3 2.5 %dynamic-slice_bitcast_fusion.1 = bf16[1024,640]{1,0:T(8,128)(2,1)} fusion(bf16[1,1024,1280]{2,1,0:T(8,128)(2,1)} %param.5, s32[]{:T(128)S(6)} %select_n.100), kind=kLoop, calls=%fused_computation.3 | loop fusion | bytes 2621444 | tf_op jit(solution)/shard_map/dynamic_slice | solution.py:293
  6.8 1.3 %collective-permute-start.3 = (bf16[512,128]{1,0:T(8,128)(2,1)S(1)}, bf16[512,128]{1,0:T(8,128)(2,1)S(1)}, u32[]{:S(2)}, u32[]{:S(2)}) collective-permute-start(bf16[512,128]{1,0:T(8,128)(2,1)S(1)} %get-tuple-element.42), channel_id=1, source_target_pairs={{0,4},{4,8},{8,12},{12,0},{1,5},{5,9},{9,13},{13,1},{2,6},{6,10},{... | collective-permute-start | bytes 393224 | tf_op jit(solution)/shard_map/ppermute | solution.py:285
  8.3 1.3 %collective-permute-start.7 = (bf16[512,128]{1,0:T(8,128)(2,1)S(1)}, bf16[512,128]{1,0:T(8,128)(2,1)S(1)}, u32[]{:S(2)}, u32[]{:S(2)}) collective-permute-start(bf16[512,128]{1,0:T(8,128)(2,1)S(1)} %get-tuple-element.40), channel_id=1, source_target_pairs={{0,4},{4,8},{8,12},{12,0},{1,5},{5,9},{9,13},{13,1},{2,6},{6,10},{... | collective-permute-start | bytes 393224 | tf_op jit(solution)/shard_map/ppermute | solution.py:285
  11.5 2.1 %collective-permute-start.5 = (bf16[512,128]{1,0:T(8,128)(2,1)S(1)}, bf16[512,128]{1,0:T(8,128)(2,1)S(1)}, u32[]{:S(2)}, u32[]{:S(2)}) collective-permute-start(bf16[512,128]{1,0:T(8,128)(2,1)S(1)} %get-tuple-element.42), channel_id=1, source_target_pairs={{0,12},{4,0},{8,4},{12,8},{1,13},{5,1},{9,5},{13,9},{2,14},{6,2},{... | collective-permute-start | bytes 393224 | tf_op jit(solution)/shard_map/ppermute | solution.py:285
  14.3 2.3 %collective-permute-start.8 = (bf16[512,128]{1,0:T(8,128)(2,1)S(1)}, bf16[512,128]{1,0:T(8,128)(2,1)S(1)}, u32[]{:S(2)}, u32[]{:S(2)}) collective-permute-start(bf16[512,128]{1,0:T(8,128)(2,1)S(1)} %get-tuple-element.40), channel_id=1, source_target_pairs={{0,8},{4,12},{8,0},{12,4},{1,9},{5,13},{9,1},{13,5},{2,10},{6,14},... | collective-permute-start | bytes 393224 | tf_op jit(solution)/shard_map/ppermute | solution.py:285
  16.6 6.6 %collective-permute-done.4 = bf16[512,128]{1,0:T(8,128)(2,1)S(1)} collective-permute-done((bf16[512,128]{1,0:T(8,128)(2,1)S(1)}, bf16[512,128]{1,0:T(8,128)(2,1)S(1)}, u32[]{:S(2)}, u32[]{:S(2)}) %collective-permute-start.4) | collective-permute-done | bytes 131104 | tf_op jit(solution)/shard_map/ppermute | solution.py:285
  23.6 2.5 %collective-permute-done.8 = bf16[512,128]{1,0:T(8,128)(2,1)S(1)} collective-permute-done((bf16[512,128]{1,0:T(8,128)(2,1)S(1)}, bf16[512,128]{1,0:T(8,128)(2,1)S(1)}, u32[]{:S(2)}, u32[]{:S(2)}) %collective-permute-start.8) | collective-permute-done | bytes 131104 | tf_op jit(solution)/shard_map/ppermute | solution.py:285
  26.1 6.5 %collective-permute-done.9 = bf16[512,128]{1,0:T(8,128)(2,1)S(1)} collective-permute-done((bf16[512,128]{1,0:T(8,128)(2,1)S(1)}, bf16[512,128]{1,0:T(8,128)(2,1)S(1)}, u32[]{:S(2)}, u32[]{:S(2)}) %collective-permute-start.9) | collective-permute-done | bytes 131104 | tf_op jit(solution)/shard_map/ppermute | solution.py:285
  33.8 17.3 %value_grad.1 = (f32[1,8,1,1280]{3,2,1,0:T(1,128)}, bf16[2048,128]{1,0:T(8,128)(2,1)}) custom-call(s32[3]{0:T(128)} %pad_add_fusion.meta, s32[16]{0:T(128)} %docs.3, bf16[1024,1280]{1,0:T(8,128)(2,1)} %bitcast.15, bf16[1024,640]{1,0:T(8,128)(2,1)} %collective-permute-done.refs_1_, bf16[1024,1280]{1,0:T(8,128)(2,1)} %bitcast.17, bf16[1024,640]{1,0:T(8,128)(2,1)} %copy-done.1, ...), custom_call_target="tpu_custom_call" | custom-call | tf_op jit(solution)/shard_map/value_grad/pallas_call | solution.py:224
  51.1 31.0 %query_grad.1 = (bf16[1024,1280]{1,0:T(8,128)(2,1)}, bf16[1024,640]{1,0:T(8,128)(2,1)}, bf16[1024,1280]{1,0:T(8,128)(2,1)}, bf16[1024,640]{1,0:T(8,128)(2,1)}, bf16[2048,128]{1,0:T(8,128)(2,1)}) custom-call(s32[3]{0:T(128)} %pad_add_fusion.meta, s32[16]{0:T(128)} %docs.3, bf16[1024,1280]{1,0:T(8,128)(2,1)} %bitcast.16, ...), custom_call_target="tpu_custom_call" | custom-call | tf_op jit(solution)/shard_map/query_grad/pallas_call | solution.py:254
  84.1 2.0 %collective-permute-start.13 = (bf16[256,128]{1,0:T(8,128)(2,1)S(1)}, bf16[256,128]{1,0:T(8,128)(2,1)S(1)}, u32[]{:S(2)}, u32[]{:S(2)}) collective-permute-start(bf16[256,128]{1,0:T(8,128)(2,1)S(1)} %get-tuple-element.35), channel_id=1, source_target_pairs={{0,8},{1,9},{4,12},{5,13},{8,0},{9,1},{12,4},{13,5},{2,10},{3,11},... | collective-permute-start | bytes 196616 | tf_op jit(solution)/shard_map/ppermute | solution.py:322
  86.1 1.4 %collective-permute-start.14 = (bf16[256,128]{1,0:T(8,128)(2,1)S(1)}, bf16[256,128]{1,0:T(8,128)(2,1)S(1)}, u32[]{:S(2)}, u32[]{:S(2)}) collective-permute-start(bf16[256,128]{1,0:T(8,128)(2,1)S(1)} %get-tuple-element.34), channel_id=1, source_target_pairs={{0,12},{1,13},{4,0},{5,1},{8,4},{9,5},{12,8},{13,9},{2,14},{3,15},... | collective-permute-start | bytes 196616 | tf_op jit(solution)/shard_map/ppermute | solution.py:322
  87.5 1.3 %collective-permute-start.15 = (bf16[256,128]{1,0:T(8,128)(2,1)S(1)}, bf16[256,128]{1,0:T(8,128)(2,1)}, u32[]{:S(2)}, u32[]{:S(2)}) collective-permute-start(bf16[256,128]{1,0:T(8,128)(2,1)S(1)} %get-tuple-element.33), channel_id=1, source_target_pairs={{0,1},{1,0},{4,5},{5,4},{8,9},{9,8},{12,13},{13,12},{2,3},{3,2},{6... | collective-permute-start | bytes 196616 | tf_op jit(solution)/shard_map/ppermute | solution.py:322
  89.4 3.0 %collective-permute-start.16 = (bf16[256,128]{1,0:T(8,128)(2,1)S(1)}, bf16[256,128]{1,0:T(8,128)(2,1)}, u32[]{:S(2)}, u32[]{:S(2)}) collective-permute-start(bf16[256,128]{1,0:T(8,128)(2,1)S(1)} %get-tuple-element.32), channel_id=1, source_target_pairs={{0,5},{1,4},{4,9},{5,8},{8,13},{9,12},{12,1},{13,0},{2,7},{3,6},{6... | collective-permute-start | bytes 196616 | tf_op jit(solution)/shard_map/ppermute | solution.py:322
  92.8 2.3 %collective-permute-start.17 = (bf16[256,128]{1,0:T(8,128)(2,1)S(1)}, bf16[256,128]{1,0:T(8,128)(2,1)}, u32[]{:S(2)}, u32[]{:S(2)}) collective-permute-start(bf16[256,128]{1,0:T(8,128)(2,1)S(1)} %get-tuple-element.31), channel_id=1, source_target_pairs={{0,9},{1,8},{4,13},{5,12},{8,1},{9,0},{12,5},{13,4},{2,11},{3,10},... | collective-permute-start | bytes 196616 | tf_op jit(solution)/shard_map/ppermute | solution.py:322
  97.0 2.2 %collective-permute-done.17 = bf16[256,128]{1,0:T(8,128)(2,1)} collective-permute-done((bf16[256,128]{1,0:T(8,128)(2,1)S(1)}, bf16[256,128]{1,0:T(8,128)(2,1)}, u32[]{:S(2)}, u32[]{:S(2)}) %collective-permute-start.17) | collective-permute-done | bytes 65568 | tf_op jit(solution)/shard_map/ppermute | solution.py:322
  99.2 2.9 %collective-permute-start.20 = (bf16[256,128]{1,0:T(8,128)(2,1)S(1)}, bf16[256,128]{1,0:T(8,128)(2,1)S(1)}, u32[]{:S(2)}, u32[]{:S(2)}) collective-permute-start(bf16[256,128]{1,0:T(8,128)(2,1)S(1)} %get-tuple-element.28), channel_id=1, source_target_pairs={{0,8},{1,9},{4,12},{5,13},{8,0},{9,1},{12,4},{13,5},{2,10},{3,11},... | collective-permute-start | bytes 196616 | tf_op jit(solution)/shard_map/ppermute | solution.py:322
  102.3 3.4 %collective-permute-done.20 = bf16[256,128]{1,0:T(8,128)(2,1)S(1)} collective-permute-done((bf16[256,128]{1,0:T(8,128)(2,1)S(1)}, bf16[256,128]{1,0:T(8,128)(2,1)S(1)}, u32[]{:S(2)}, u32[]{:S(2)}) %collective-permute-start.20) | collective-permute-done | bytes 65568 | tf_op jit(solution)/shard_map/ppermute | solution.py:322
  106.4 1.7 %collective-permute-done.21 = bf16[256,128]{1,0:T(8,128)(2,1)S(1)} collective-permute-done((bf16[256,128]{1,0:T(8,128)(2,1)S(1)}, bf16[256,128]{1,0:T(8,128)(2,1)S(1)}, u32[]{:S(2)}, u32[]{:S(2)}) %collective-permute-start.21) | collective-permute-done | bytes 65568 | tf_op jit(solution)/shard_map/ppermute | solution.py:322
  108.1 2.1 %collective-permute-start.24 = (bf16[256,128]{1,0:T(8,128)(2,1)S(1)}, bf16[256,128]{1,0:T(8,128)(2,1)}, u32[]{:S(2)}, u32[]{:S(2)}) collective-permute-start(bf16[256,128]{1,0:T(8,128)(2,1)S(1)} %get-tuple-element.24), channel_id=1, source_target_pairs={{0,9},{1,8},{4,13},{5,12},{8,1},{9,0},{12,5},{13,4},{2,11},{3,10},... | collective-permute-start | bytes 196616 | tf_op jit(solution)/shard_map/ppermute | solution.py:322
  111.6 2.9 %collective-permute-done.24 = bf16[256,128]{1,0:T(8,128)(2,1)} collective-permute-done((bf16[256,128]{1,0:T(8,128)(2,1)S(1)}, bf16[256,128]{1,0:T(8,128)(2,1)}, u32[]{:S(2)}, u32[]{:S(2)}) %collective-permute-start.24) | collective-permute-done | bytes 65568 | tf_op jit(solution)/shard_map/ppermute | solution.py:322
  114.6 1.9 %collective-permute-done.25 = bf16[256,128]{1,0:T(8,128)(2,1)} collective-permute-done((bf16[256,128]{1,0:T(8,128)(2,1)S(1)}, bf16[256,128]{1,0:T(8,128)(2,1)}, u32[]{:S(2)}, u32[]{:S(2)}) %collective-permute-start.25) | collective-permute-done | bytes 65568 | tf_op jit(solution)/shard_map/ppermute | solution.py:322
  116.4 1.3 %broadcast_select_fusion.1 = (f32[256,128]{1,0:T(8,128)S(1)}, f32[256,128]{1,0:T(8,128)S(1)}, f32[256,128]{1,0:T(8,128)S(1)}, f32[256,128]{1,0:T(8,128)S(1)}) fusion(pred[]{:T(512)S(6)} %eq.2, bf16[256,128]{1,0:T(8,128)(2,1)} %collective-permute-done.25, bf16[256,128]{1,0:T(8,128)(2,1)} %collective-permute-done.24, ...), kind=kLoop, calls=%fused_computation.13 | loop fusion | flops 1048576 | bytes 1572869 | tf_op jit(solution)/shard_map/jit(_where)/select_n | solution.py:326
  120.6 1.5 %copy-done.13 = bf16[1,1024,1280]{2,1,0:T(8,128)(2,1)} copy-done((bf16[1,1024,1280]{2,1,0:T(8,128)(2,1)}, bf16[1,1024,1280]{2,1,0:T(8,128)(2,1)S(1)}, u32[]{:S(2)}) %copy-start.13) | copy-done | bytes 2621464
  (82 shorter events, 17.8 us)
Async XLA Ops:
  1.6 5.0 %collective-permute-start.2 = (bf16[256,128]{1,0:T(8,128)(2,1)S(1)}, bf16[256,128]{1,0:T(8,128)(2,1)S(1)}, u32[]{:S(2)}, u32[]{:S(2)}) collective-permute-start(bf16[256,128]{1,0:T(8,128)(2,1)S(1)} %constant_dynamic-slice_fusion.15), channel_id=1, source_target_pairs={{0,1},{1,0},{2,3},{3,2},{4,5},{5,4},{6,7},{7,6},{8,9},{9,8},{10,11... | collective-permute-start | bytes 196616 | tf_op jit(solution)/shard_map/ppermute | solution.py:297
  4.9 27.8 %collective-permute-start = (bf16[1024,640]{1,0:T(8,128)(2,1)}, bf16[1024,640]{1,0:T(8,128)(2,1)}, u32[]{:S(2)}, u32[]{:S(2)}) collective-permute-start(bf16[1024,640]{1,0:T(8,128)(2,1)} %dynamic-slice_bitcast_fusion.1), channel_id=1, source_target_pairs={{0,1},{1,0},{2,3},{3,2},{4,5},{5,4},{6,7},{7,6},{8,9},{9,8},{10,11... | collective-permute-start | bytes 3932168 | tf_op jit(solution)/shard_map/ppermute | solution.py:297
  6.0 26.6 %collective-permute-start.1 = (bf16[1024,640]{1,0:T(8,128)(2,1)}, bf16[1024,640]{1,0:T(8,128)(2,1)S(1)}, u32[]{:S(2)}, u32[]{:S(2)}) collective-permute-start(bf16[1024,640]{1,0:T(8,128)(2,1)} %dynamic-slice_bitcast_fusion), channel_id=1, source_target_pairs={{0,1},{1,0},{2,3},{3,2},{4,5},{5,4},{6,7},{7,6},{8,9},{9,8},{10,11... | collective-permute-start | bytes 3932168 | tf_op jit(solution)/shard_map/ppermute | solution.py:297
  6.8 4.7 %collective-permute-start.3 = (bf16[512,128]{1,0:T(8,128)(2,1)S(1)}, bf16[512,128]{1,0:T(8,128)(2,1)S(1)}, u32[]{:S(2)}, u32[]{:S(2)}) collective-permute-start(bf16[512,128]{1,0:T(8,128)(2,1)S(1)} %get-tuple-element.42), channel_id=1, source_target_pairs={{0,4},{4,8},{8,12},{12,0},{1,5},{5,9},{9,13},{13,1},{2,6},{6,10},{... | collective-permute-start | bytes 393224 | tf_op jit(solution)/shard_map/ppermute | solution.py:285
  8.3 6.0 %collective-permute-start.7 = (bf16[512,128]{1,0:T(8,128)(2,1)S(1)}, bf16[512,128]{1,0:T(8,128)(2,1)S(1)}, u32[]{:S(2)}, u32[]{:S(2)}) collective-permute-start(bf16[512,128]{1,0:T(8,128)(2,1)S(1)} %get-tuple-element.40), channel_id=1, source_target_pairs={{0,4},{4,8},{8,12},{12,0},{1,5},{5,9},{9,13},{13,1},{2,6},{6,10},{... | collective-permute-start | bytes 393224 | tf_op jit(solution)/shard_map/ppermute | solution.py:285
  10.3 12.9 %collective-permute-start.4 = (bf16[512,128]{1,0:T(8,128)(2,1)S(1)}, bf16[512,128]{1,0:T(8,128)(2,1)S(1)}, u32[]{:S(2)}, u32[]{:S(2)}) collective-permute-start(bf16[512,128]{1,0:T(8,128)(2,1)S(1)} %get-tuple-element.42), channel_id=1, source_target_pairs={{0,8},{4,12},{8,0},{12,4},{1,9},{5,13},{9,1},{13,5},{2,10},{6,14},... | collective-permute-start | bytes 393224 | tf_op jit(solution)/shard_map/ppermute | solution.py:285
  11.5 14.6 %collective-permute-start.5 = (bf16[512,128]{1,0:T(8,128)(2,1)S(1)}, bf16[512,128]{1,0:T(8,128)(2,1)S(1)}, u32[]{:S(2)}, u32[]{:S(2)}) collective-permute-start(bf16[512,128]{1,0:T(8,128)(2,1)S(1)} %get-tuple-element.42), channel_id=1, source_target_pairs={{0,12},{4,0},{8,4},{12,8},{1,13},{5,1},{9,5},{13,9},{2,14},{6,2},{... | collective-permute-start | bytes 393224 | tf_op jit(solution)/shard_map/ppermute | solution.py:285
  14.3 11.7 %collective-permute-start.8 = (bf16[512,128]{1,0:T(8,128)(2,1)S(1)}, bf16[512,128]{1,0:T(8,128)(2,1)S(1)}, u32[]{:S(2)}, u32[]{:S(2)}) collective-permute-start(bf16[512,128]{1,0:T(8,128)(2,1)S(1)} %get-tuple-element.40), channel_id=1, source_target_pairs={{0,8},{4,12},{8,0},{12,4},{1,9},{5,13},{9,1},{13,5},{2,10},{6,14},... | collective-permute-start | bytes 393224 | tf_op jit(solution)/shard_map/ppermute | solution.py:285
  23.2 9.4 %collective-permute-start.9 = (bf16[512,128]{1,0:T(8,128)(2,1)S(1)}, bf16[512,128]{1,0:T(8,128)(2,1)S(1)}, u32[]{:S(2)}, u32[]{:S(2)}) collective-permute-start(bf16[512,128]{1,0:T(8,128)(2,1)S(1)} %get-tuple-element.40), channel_id=1, source_target_pairs={{0,12},{4,0},{8,4},{12,8},{1,13},{5,1},{9,5},{13,9},{2,14},{6,2},{... | collective-permute-start | bytes 393224 | tf_op jit(solution)/shard_map/ppermute | solution.py:285
  82.1 37.1 %collective-permute-start.11 = (bf16[1024,640]{1,0:T(8,128)(2,1)}, bf16[1024,640]{1,0:T(8,128)(2,1)S(1)}, u32[]{:S(2)}, u32[]{:S(2)}) collective-permute-start(bf16[1024,640]{1,0:T(8,128)(2,1)} %get-tuple-element.15), channel_id=1, source_target_pairs={{0,1},{1,0},{2,3},{3,2},{4,5},{5,4},{6,7},{7,6},{8,9},{9,8},{10,11... | collective-permute-start | bytes 3932168 | tf_op jit(solution)/shard_map/ppermute | solution.py:297
  82.9 37.5 %collective-permute-start.10 = (bf16[1024,640]{1,0:T(8,128)(2,1)}, bf16[1024,640]{1,0:T(8,128)(2,1)S(1)}, u32[]{:S(2)}, u32[]{:S(2)}) collective-permute-start(bf16[1024,640]{1,0:T(8,128)(2,1)} %get-tuple-element.13), channel_id=1, source_target_pairs={{0,1},{1,0},{2,3},{3,2},{4,5},{5,4},{6,7},{7,6},{8,9},{9,8},{10,11... | collective-permute-start | bytes 3932168 | tf_op jit(solution)/shard_map/ppermute | solution.py:297
  84.1 5.3 %collective-permute-start.13 = (bf16[256,128]{1,0:T(8,128)(2,1)S(1)}, bf16[256,128]{1,0:T(8,128)(2,1)S(1)}, u32[]{:S(2)}, u32[]{:S(2)}) collective-permute-start(bf16[256,128]{1,0:T(8,128)(2,1)S(1)} %get-tuple-element.35), channel_id=1, source_target_pairs={{0,8},{1,9},{4,12},{5,13},{8,0},{9,1},{12,4},{13,5},{2,10},{3,11},... | collective-permute-start | bytes 196616 | tf_op jit(solution)/shard_map/ppermute | solution.py:322
  86.1 6.7 %collective-permute-start.14 = (bf16[256,128]{1,0:T(8,128)(2,1)S(1)}, bf16[256,128]{1,0:T(8,128)(2,1)S(1)}, u32[]{:S(2)}, u32[]{:S(2)}) collective-permute-start(bf16[256,128]{1,0:T(8,128)(2,1)S(1)} %get-tuple-element.34), channel_id=1, source_target_pairs={{0,12},{1,13},{4,0},{5,1},{8,4},{9,5},{12,8},{13,9},{2,14},{3,15},... | collective-permute-start | bytes 196616 | tf_op jit(solution)/shard_map/ppermute | solution.py:322
  87.5 7.6 %collective-permute-start.15 = (bf16[256,128]{1,0:T(8,128)(2,1)S(1)}, bf16[256,128]{1,0:T(8,128)(2,1)}, u32[]{:S(2)}, u32[]{:S(2)}) collective-permute-start(bf16[256,128]{1,0:T(8,128)(2,1)S(1)} %get-tuple-element.33), channel_id=1, source_target_pairs={{0,1},{1,0},{4,5},{5,4},{8,9},{9,8},{12,13},{13,12},{2,3},{3,2},{6... | collective-permute-start | bytes 196616 | tf_op jit(solution)/shard_map/ppermute | solution.py:322
  89.4 6.9 %collective-permute-start.16 = (bf16[256,128]{1,0:T(8,128)(2,1)S(1)}, bf16[256,128]{1,0:T(8,128)(2,1)}, u32[]{:S(2)}, u32[]{:S(2)}) collective-permute-start(bf16[256,128]{1,0:T(8,128)(2,1)S(1)} %get-tuple-element.32), channel_id=1, source_target_pairs={{0,5},{1,4},{4,9},{5,8},{8,13},{9,12},{12,1},{13,0},{2,7},{3,6},{6... | collective-permute-start | bytes 196616 | tf_op jit(solution)/shard_map/ppermute | solution.py:322
  92.8 6.5 %collective-permute-start.17 = (bf16[256,128]{1,0:T(8,128)(2,1)S(1)}, bf16[256,128]{1,0:T(8,128)(2,1)}, u32[]{:S(2)}, u32[]{:S(2)}) collective-permute-start(bf16[256,128]{1,0:T(8,128)(2,1)S(1)} %get-tuple-element.31), channel_id=1, source_target_pairs={{0,9},{1,8},{4,13},{5,12},{8,1},{9,0},{12,5},{13,4},{2,11},{3,10},... | collective-permute-start | bytes 196616 | tf_op jit(solution)/shard_map/ppermute | solution.py:322
  95.0 7.1 %collective-permute-start.18 = (bf16[256,128]{1,0:T(8,128)(2,1)S(1)}, bf16[256,128]{1,0:T(8,128)(2,1)S(1)}, u32[]{:S(2)}, u32[]{:S(2)}) collective-permute-start(bf16[256,128]{1,0:T(8,128)(2,1)S(1)} %get-tuple-element.30), channel_id=1, source_target_pairs={{0,13},{1,12},{4,1},{5,0},{8,5},{9,4},{12,9},{13,8},{2,15},{3,14},... | collective-permute-start | bytes 196616 | tf_op jit(solution)/shard_map/ppermute | solution.py:322
  96.3 5.9 %collective-permute-start.19 = (bf16[256,128]{1,0:T(8,128)(2,1)S(1)}, bf16[256,128]{1,0:T(8,128)(2,1)S(1)}, u32[]{:S(2)}, u32[]{:S(2)}) collective-permute-start(bf16[256,128]{1,0:T(8,128)(2,1)S(1)} %get-tuple-element.22), channel_id=1, source_target_pairs={{0,4},{1,5},{4,8},{5,9},{8,12},{9,13},{12,0},{13,1},{2,6},{3,7},{6... | collective-permute-start | bytes 196616 | tf_op jit(solution)/shard_map/ppermute | solution.py:322
  99.2 6.5 %collective-permute-start.20 = (bf16[256,128]{1,0:T(8,128)(2,1)S(1)}, bf16[256,128]{1,0:T(8,128)(2,1)S(1)}, u32[]{:S(2)}, u32[]{:S(2)}) collective-permute-start(bf16[256,128]{1,0:T(8,128)(2,1)S(1)} %get-tuple-element.28), channel_id=1, source_target_pairs={{0,8},{1,9},{4,12},{5,13},{8,0},{9,1},{12,4},{13,5},{2,10},{3,11},... | collective-permute-start | bytes 196616 | tf_op jit(solution)/shard_map/ppermute | solution.py:322
  102.2 5.9 %collective-permute-start.21 = (bf16[256,128]{1,0:T(8,128)(2,1)S(1)}, bf16[256,128]{1,0:T(8,128)(2,1)S(1)}, u32[]{:S(2)}, u32[]{:S(2)}) collective-permute-start(bf16[256,128]{1,0:T(8,128)(2,1)S(1)} %get-tuple-element.27), channel_id=1, source_target_pairs={{0,12},{1,13},{4,0},{5,1},{8,4},{9,5},{12,8},{13,9},{2,14},{3,15},... | collective-permute-start | bytes 196616 | tf_op jit(solution)/shard_map/ppermute | solution.py:322
  102.2 8.1 %collective-permute-start.22 = (bf16[256,128]{1,0:T(8,128)(2,1)S(1)}, bf16[256,128]{1,0:T(8,128)(2,1)S(1)}, u32[]{:S(2)}, u32[]{:S(2)}) collective-permute-start(bf16[256,128]{1,0:T(8,128)(2,1)S(1)} %get-tuple-element.26), channel_id=1, source_target_pairs={{0,1},{1,0},{4,5},{5,4},{8,9},{9,8},{12,13},{13,12},{2,3},{3,2},{6... | collective-permute-start | bytes 196616 | tf_op jit(solution)/shard_map/ppermute | solution.py:322
  105.7 6.0 %collective-permute-start.23 = (bf16[256,128]{1,0:T(8,128)(2,1)S(1)}, bf16[256,128]{1,0:T(8,128)(2,1)}, u32[]{:S(2)}, u32[]{:S(2)}) collective-permute-start(bf16[256,128]{1,0:T(8,128)(2,1)S(1)} %get-tuple-element.25), channel_id=1, source_target_pairs={{0,5},{1,4},{4,9},{5,8},{8,13},{9,12},{12,1},{13,0},{2,7},{3,6},{6... | collective-permute-start | bytes 196616 | tf_op jit(solution)/shard_map/ppermute | solution.py:322
  108.1 6.5 %collective-permute-start.24 = (bf16[256,128]{1,0:T(8,128)(2,1)S(1)}, bf16[256,128]{1,0:T(8,128)(2,1)}, u32[]{:S(2)}, u32[]{:S(2)}) collective-permute-start(bf16[256,128]{1,0:T(8,128)(2,1)S(1)} %get-tuple-element.24), channel_id=1, source_target_pairs={{0,9},{1,8},{4,13},{5,12},{8,1},{9,0},{12,5},{13,4},{2,11},{3,10},... | collective-permute-start | bytes 196616 | tf_op jit(solution)/shard_map/ppermute | solution.py:322
  110.9 5.5 %collective-permute-start.25 = (bf16[256,128]{1,0:T(8,128)(2,1)S(1)}, bf16[256,128]{1,0:T(8,128)(2,1)}, u32[]{:S(2)}, u32[]{:S(2)}) collective-permute-start(bf16[256,128]{1,0:T(8,128)(2,1)S(1)} %get-tuple-element.23), channel_id=1, source_target_pairs={{0,13},{1,12},{4,1},{5,0},{8,5},{9,4},{12,9},{13,8},{2,15},{3,14},... | collective-permute-start | bytes 196616 | tf_op jit(solution)/shard_map/ppermute | solution.py:322
  (16 other events, 119.1 us)

commit v2 on v1

--- a/solution.py
+++ b/solution.py
@@ -272,23 +272,6 @@
     return outs[:parts], outs[parts:2 * parts], outs[-1]
 
 
-def shift_perm(depth_count, hops):
-    return [(d, (d + hops) % depth_count) for d in range(depth_count)]
-
-
-def gather_depth(rows, depth_count):
-    me = lax.axis_index("depth")
-    count = rows.shape[0]
-    full = jnp.zeros((count * depth_count, rows.shape[1]), rows.dtype)
-    pieces = [(0, rows)]
-    for hops in range(1, depth_count):
-        pieces.append((hops, lax.ppermute(rows, "depth", shift_perm(depth_count, hops))))
-    for hops, piece in pieces:
-        source = lax.rem(me - hops + depth_count, depth_count)
-        full = lax.dynamic_update_slice(full, piece, (source * count, 0))
-    return full
-
-
 def head_columns(rows, which, width):
     return lax.dynamic_slice(rows, (0, which * width), (rows.shape[0], width))
 
@@ -297,44 +280,34 @@
     return lax.ppermute(array, "dp", [(0, 1), (1, 0)])
 
 
-def spread_heads(rows, core, width):
-    own = head_columns(rows, core, width)
-    other = swap_cores(head_columns(rows, 1 - core, width))
-    first = core == 0
-    return jnp.concatenate([jnp.where(first, own, other), jnp.where(first, other, own)], axis=0)
-
-
-def return_terms(terms, depth_count, core):
-    me = lax.axis_index("depth")
+def exchange(array):
+    return lax.all_to_all(array, ("depth", "dp"), 0, 0, tiled=True)
+
+
+def gather_heads(rows, depth_count):
+    shard, width = rows.shape
+    pieces = jnp.transpose(rows.reshape(shard, 2, width // 2), (1, 0, 2))
+    pieces = jnp.broadcast_to(pieces[None], (depth_count,) + pieces.shape)
+    full = exchange(pieces.reshape(2 * depth_count, shard, width // 2))
+    return full.reshape(2 * depth_count * shard, width // 2)
+
+
+def return_terms(terms, depth_count):
     shard = terms.shape[0] // (2 * depth_count)
-    sums = [[], []]
-    for hops in range(depth_count):
-        target = lax.rem(me + hops, depth_count)
-        for flip in range(2):
-            side = core if flip == 0 else 1 - core
-            piece = lax.dynamic_slice(terms, ((2 * target + side) * shard, 0), (shard, terms.shape[1]))
-            if hops or flip:
-                perm = [
-                    (2 * d + c, 2 * ((d + hops) % depth_count) + (c ^ flip))
-                    for d in range(depth_count)
-                    for c in range(2)
-                ]
-                piece = lax.ppermute(piece, ("depth", "dp"), perm)
-            sums[flip].append(piece.astype(jnp.float32))
-    own, other = sum(sums[0]), sum(sums[1])
-    first = core == 0
-    return jnp.concatenate([jnp.where(first, own, other), jnp.where(first, other, own)], axis=1)
+    got = exchange(terms.reshape(2 * depth_count, shard, terms.shape[1]))
+    got = got.reshape(depth_count, 2, shard, terms.shape[1])
+    summed = jnp.sum(got.astype(jnp.float32), axis=0)
+    return jnp.transpose(summed, (1, 0, 2)).reshape(shard, 2 * terms.shape[1])
 
 
 def by_head(queries, grad_out, key_rows, value_rows, doc_starts):
     depth_count = lax.axis_size("depth")
     core = lax.axis_index("dp")
     local_blocks = queries.shape[0] // QB
-    kv_width = key_rows.shape[1] // 2
     query_width = queries.shape[1] // 2
-    heads = kv_width // HEAD_DIM
-    keys = gather_depth(spread_heads(key_rows, core, kv_width), depth_count)
-    values = gather_depth(spread_heads(value_rows, core, kv_width), depth_count)
+    heads = key_rows.shape[1] // (2 * HEAD_DIM)
+    keys = gather_heads(key_rows, depth_count)
+    values = gather_heads(value_rows, depth_count)
     query_got = swap_cores(head_columns(queries, 1 - core, query_width))
     grad_got = swap_cores(head_columns(grad_out, 1 - core, query_width))
     meta = jnp.stack([core * heads, core * local_blocks, (1 - core) * local_blocks]).astype(jnp.int32)
@@ -344,8 +317,8 @@
     attns, query_grads, key_terms = run_query(
         meta, doc_starts, query_parts, grad_parts, keys, values, totals, 2, 3
     )
-    value_grad = return_terms(value_terms, depth_count, core)
-    key_grad = return_terms(key_terms, depth_count, core)
+    value_grad = return_terms(value_terms, depth_count)
+    key_grad = return_terms(key_terms, depth_count)
     outs = []
     for own, send in (attns, query_grads):
         outs.append(lax.dynamic_update_slice(own, swap_cores(send), (0, (1 - core) * query_width)))

time: 123 us -> 113 us (0.919)
  the two profiles are of different devices: /device:TPU:13 before, /device:TPU:0 now
where the time goes in v2:
time: 113 us; the launch traced here: 111 us
  Pallas kernels  48.1 us (43%)
  waiting for transfers between devices  24.9 us (22%)
  starting transfers between devices  21.2 us (19%)
  local copies, waits for them, and re-layouts  15 us (13%)
    pallas_call x1, Pallas kernels, run_query(): pl.pallas_call(functools.partial(query_kernel, local_blocks, parts, count...  30.8 us
    all_to_all x4, waiting for transfers between devices, exchange(): return lax.all_to_all(array, ('depth', 'dp'), 0, 0, tiled=True)  24.9 us
    all_to_all x4, starting transfers between devices, exchange(): return lax.all_to_all(array, ('depth', 'dp'), 0, 0, tiled=True)  19.6 us
    pallas_call x1, Pallas kernels, run_value(): pl.pallas_call(functools.partial(value_kernel, local_blocks, parts, count...  17.2 us
    unnamed x16, local copies, waits for them, and re-layouts  5.27 us
    dynamic_slice x2, local copies, waits for them, and re-layouts, head_columns(): return lax.dynamic_slice(rows, (0, which * width), (rows.shape[0], width))  3.69 us
    dynamic_update_slice x2, local copies, waits for them, and re-layouts, by_head(): lax.dynamic_update_slice(own, swap_cores(send), (0, (1 - core) * query_wi...  2.71 us
  transfers between devices with their start and end apart: 8, of which 2 were waited for; matrix products, arithmetic and copies ran while one was open for 8% of the time, Pallas kernels for 43%

profile of v2, /device:TPU:0, one launch (start us, length us, event | category | flops | bytes accessed | tf_op | source)
XLA Modules:
  0.0 110.7 jit_solution(13128581374169474919)
XLA Ops:
  0.6 1.1 reshape.52
  1.8 0.9 broadcast_in_dim.22
  2.6 6.3 %all-to-all-start = ((bf16[8,256,128]{2,1,0:T(8,128)(2,1)}), bf16[8,256,128]{2,1,0:T(8,128)(2,1)S(1)}, u32[]{:S(2)}, u32[]{:S(2)}) async-start(bf16[8,256,128]{2,1,0:T(8,128)(2,1)} %bitcast.37), calls=%async_computation | async-start | bytes 1048576 | tf_op jit(solution)/shard_map/all_to_all | solution.py:284
  9.0 2.5 %dynamic-slice_bitcast_fusion = bf16[1024,640]{1,0:T(8,128)(2,1)} fusion(bf16[1,1024,1280]{2,1,0:T(8,128)(2,1)} %param.6, s32[]{:T(128)S(6)} %select_n.2), kind=kLoop, calls=%fused_computation.2 | loop fusion | bytes 2621444 | tf_op jit(solution)/shard_map/dynamic_slice | solution.py:276
  11.5 0.5 collective-permute-start.1
  12.0 1.2 %dynamic-slice_bitcast_fusion.1 = bf16[1024,640]{1,0:T(8,128)(2,1)} fusion(bf16[1,1024,1280]{2,1,0:T(8,128)(2,1)S(1)} %copy-done, s32[]{:T(128)S(6)} %select_n.2), kind=kLoop, calls=%fused_computation.3 | loop fusion | bytes 2621444 | tf_op jit(solution)/shard_map/dynamic_slice | solution.py:276
  13.3 11.1 %all-to-all-done = bf16[8,256,128]{2,1,0:T(8,128)(2,1)S(1)} async-done(((bf16[8,256,128]{2,1,0:T(8,128)(2,1)}), bf16[8,256,128]{2,1,0:T(8,128)(2,1)S(1)}, u32[]{:S(2)}, u32[]{:S(2)}) %all-to-all-start) | async-done | bytes 524320 | tf_op jit(solution)/shard_map/all_to_all | solution.py:284
  24.3 1.0 broadcast_in_dim.23
  25.3 3.5 %all-to-all-start.1 = ((bf16[8,256,128]{2,1,0:T(8,128)(2,1)}), bf16[8,256,128]{2,1,0:T(8,128)(2,1)S(1)}, u32[]{:S(2)}, u32[]{:S(2)}) async-start(bf16[8,256,128]{2,1,0:T(8,128)(2,1)} %bitcast.11), calls=%async_computation.1 | async-start | bytes 1048576 | tf_op jit(solution)/shard_map/all_to_all | solution.py:284
  28.8 0.7 pad_add_fusion.meta
  29.5 1.1 copy-done.1
  30.5 17.2 %value_grad.1 = (f32[1,8,1,1280]{3,2,1,0:T(1,128)}, bf16[2048,128]{1,0:T(8,128)(2,1)}) custom-call(s32[3]{0:T(128)} %pad_add_fusion.meta, s32[16]{0:T(128)} %docs.3, bf16[1024,1280]{1,0:T(8,128)(2,1)} %bitcast.31, bf16[1024,640]{1,0:T(8,128)(2,1)} %copy-done.1, bf16[1024,1280]{1,0:T(8,128)(2,1)} %bitcast.33, ...), custom_call_target="tpu_custom_call" | custom-call | tf_op jit(solution)/shard_map/value_grad/pallas_call | solution.py:224
  47.8 5.0 %all-to-all-start.3 = ((bf16[8,256,128]{2,1,0:T(8,128)(2,1)}), bf16[8,256,128]{2,1,0:T(8,128)(2,1)S(1)}, u32[]{:S(2)}, u32[]{:S(2)}) async-start(bf16[8,256,128]{2,1,0:T(8,128)(2,1)} %bitcast.46), calls=%async_computation.3 | async-start | bytes 1048576 | tf_op jit(solution)/shard_map/all_to_all | solution.py:284
  52.9 30.8 %query_grad.1 = (bf16[1024,1280]{1,0:T(8,128)(2,1)}, bf16[1024,640]{1,0:T(8,128)(2,1)}, bf16[1024,1280]{1,0:T(8,128)(2,1)}, bf16[1024,640]{1,0:T(8,128)(2,1)}, bf16[2048,128]{1,0:T(8,128)(2,1)}) custom-call(s32[3]{0:T(128)} %pad_add_fusion.meta, s32[16]{0:T(128)} %docs.3, bf16[1024,1280]{1,0:T(8,128)(2,1)} %bitcast.32, bf16[1024,640]{1,0:T(8,128)(2,1)} %copy-done.1, ...), custom_call_target="tpu_custom_call" | custom-call | tf_op jit(solution)/shard_map/query_grad/pallas_call | solution.py:254
  83.7 0.6 collective-permute-start.2
  84.3 4.8 %all-to-all-start.2 = ((bf16[8,256,128]{2,1,0:T(8,128)(2,1)}), bf16[8,256,128]{2,1,0:T(8,128)(2,1)S(1)}, u32[]{:S(2)}, u32[]{:S(2)}) async-start(bf16[8,256,128]{2,1,0:T(8,128)(2,1)} %bitcast.45), calls=%async_computation.2 | async-start | bytes 1048576 | tf_op jit(solution)/shard_map/all_to_all | solution.py:284
  89.0 0.5 collective-permute-start.3
  89.7 0.8 copy.18
  90.6 13.8 %all-to-all-done.2 = bf16[8,256,128]{2,1,0:T(8,128)(2,1)S(1)} async-done(((bf16[8,256,128]{2,1,0:T(8,128)(2,1)}), bf16[8,256,128]{2,1,0:T(8,128)(2,1)S(1)}, u32[]{:S(2)}, u32[]{:S(2)}) %all-to-all-start.2) | async-done | bytes 524320 | tf_op jit(solution)/shard_map/all_to_all | solution.py:284
  104.6 0.8 copy.17
  105.4 1.2 %bitcast_dynamic-update-slice_fusion.1 = bf16[1,1024,1280]{2,1,0:T(8,128)(2,1)} fusion(bf16[1,1024,1280]{2,1,0:T(8,128)(2,1)} %bitcast.50, s32[]{:T(128)S(6)} %select_n.2, bf16[1024,640]{1,0:T(8,128)(2,1)S(1)} %collective-permute-done.2), kind=kLoop, calls=%fused_computation.1 | loop fusion | bytes 2621444 | tf_op jit(solution)/shard_map/dynamic_update_slice | solution.py:324
  106.6 1.0 copy-done.5
  107.6 1.5 %bitcast_dynamic-update-slice_fusion = bf16[1,1024,1280]{2,1,0:T(8,128)(2,1)S(1)} fusion(bf16[1,1024,1280]{2,1,0:T(8,128)(2,1)S(1)} %bitcast.49, s32[]{:T(128)S(6)} %select_n.2, bf16[1024,640]{1,0:T(8,128)(2,1)} %collective-permute-done.3), kind=kLoop, calls=%fused_computation | loop fusion | bytes 2621444 | tf_op jit(solution)/shard_map/dynamic_update_slice | solution.py:324
  109.2 1.5 %copy-done.6 = bf16[1,1024,1280]{2,1,0:T(8,128)(2,1)} copy-done((bf16[1,1024,1280]{2,1,0:T(8,128)(2,1)}, bf16[1,1024,1280]{2,1,0:T(8,128)(2,1)S(1)}, u32[]{:S(2)}) %copy-start.6) | copy-done | bytes 2621464
  (25 shorter events, 0.5 us)
Async XLA Ops:
  0.6 11.4 %copy-start = (bf16[1,1024,1280]{2,1,0:T(8,128)(2,1)S(1)}, bf16[1,1024,1280]{2,1,0:T(8,128)(2,1)}, u32[]{:S(2)}) copy-start(bf16[1,1024,1280]{2,1,0:T(8,128)(2,1)} %param.5) | copy-start | bytes 7864324
  2.6 21.7 %all-to-all-start = ((bf16[8,256,128]{2,1,0:T(8,128)(2,1)}), bf16[8,256,128]{2,1,0:T(8,128)(2,1)S(1)}, u32[]{:S(2)}, u32[]{:S(2)}) async-start(bf16[8,256,128]{2,1,0:T(8,128)(2,1)} %bitcast.37), calls=%async_computation | async-start | bytes 1048576 | tf_op jit(solution)/shard_map/all_to_all | solution.py:284
  9.0 4.2 %copy-start.4 = (bf16[256,256]{1,0:T(8,128)(2,1)S(1)}, bf16[256,256]{1,0:T(8,128)(2,1)}, u32[]{:S(2)}) copy-start(bf16[256,256]{1,0:T(8,128)(2,1)} %param.8) | copy-start | bytes 393220
  11.5 18.0 %collective-permute-start.1 = (bf16[1024,640]{1,0:T(8,128)(2,1)}, bf16[1024,640]{1,0:T(8,128)(2,1)}, u32[]{:S(2)}, u32[]{:S(2)}) collective-permute-start(bf16[1024,640]{1,0:T(8,128)(2,1)} %dynamic-slice_bitcast_fusion), channel_id=1, source_target_pairs={{0,1},{1,0},{2,3},{3,2},{4,5},{5,4},{6,7},{7,6},{8,9},{9,8},{10,11... | collective-permute-start | bytes 3932168 | tf_op jit(solution)/shard_map/ppermute | solution.py:280
  13.2 16.3 %collective-permute-start = (bf16[1024,640]{1,0:T(8,128)(2,1)}, bf16[1024,640]{1,0:T(8,128)(2,1)S(1)}, u32[]{:S(2)}, u32[]{:S(2)}) collective-permute-start(bf16[1024,640]{1,0:T(8,128)(2,1)} %dynamic-slice_bitcast_fusion.1), channel_id=1, source_target_pairs={{0,1},{1,0},{2,3},{3,2},{4,5},{5,4},{6,7},{7,6},{8,9},{9,8},{10,11... | collective-permute-start | bytes 3932168 | tf_op jit(solution)/shard_map/ppermute | solution.py:280
  24.3 5.1 %copy-start.2 = (bf16[8,256,128]{2,1,0:T(8,128)(2,1)}, bf16[8,256,128]{2,1,0:T(8,128)(2,1)S(1)}, u32[]{:S(2)}) copy-start(bf16[8,256,128]{2,1,0:T(8,128)(2,1)S(1)} %all-to-all-done) | copy-start | bytes 1572868
  25.3 22.5 %all-to-all-start.1 = ((bf16[8,256,128]{2,1,0:T(8,128)(2,1)}), bf16[8,256,128]{2,1,0:T(8,128)(2,1)S(1)}, u32[]{:S(2)}, u32[]{:S(2)}) async-start(bf16[8,256,128]{2,1,0:T(8,128)(2,1)} %bitcast.11), calls=%async_computation.1 | async-start | bytes 1048576 | tf_op jit(solution)/shard_map/all_to_all | solution.py:284
  29.5 1.1 copy-start.1
  47.8 5.1 %copy-start.3 = (bf16[8,256,128]{2,1,0:T(8,128)(2,1)}, bf16[8,256,128]{2,1,0:T(8,128)(2,1)S(1)}, u32[]{:S(2)}) copy-start(bf16[8,256,128]{2,1,0:T(8,128)(2,1)S(1)} %all-to-all-done.1) | copy-start | bytes 1572868
  47.8 36.5 %all-to-all-start.3 = ((bf16[8,256,128]{2,1,0:T(8,128)(2,1)}), bf16[8,256,128]{2,1,0:T(8,128)(2,1)S(1)}, u32[]{:S(2)}, u32[]{:S(2)}) async-start(bf16[8,256,128]{2,1,0:T(8,128)(2,1)} %bitcast.46), calls=%async_computation.3 | async-start | bytes 1048576 | tf_op jit(solution)/shard_map/all_to_all | solution.py:284
  83.7 21.7 %collective-permute-start.2 = (bf16[1024,640]{1,0:T(8,128)(2,1)}, bf16[1024,640]{1,0:T(8,128)(2,1)S(1)}, u32[]{:S(2)}, u32[]{:S(2)}) collective-permute-start(bf16[1024,640]{1,0:T(8,128)(2,1)} %get-tuple-element.13), channel_id=1, source_target_pairs={{0,1},{1,0},{2,3},{3,2},{4,5},{5,4},{6,7},{7,6},{8,9},{9,8},{10,11... | collective-permute-start | bytes 3932168 | tf_op jit(solution)/shard_map/ppermute | solution.py:280
  84.3 20.1 %all-to-all-start.2 = ((bf16[8,256,128]{2,1,0:T(8,128)(2,1)}), bf16[8,256,128]{2,1,0:T(8,128)(2,1)S(1)}, u32[]{:S(2)}, u32[]{:S(2)}) async-start(bf16[8,256,128]{2,1,0:T(8,128)(2,1)} %bitcast.45), calls=%async_computation.2 | async-start | bytes 1048576 | tf_op jit(solution)/shard_map/all_to_all | solution.py:284
  89.0 17.6 %collective-permute-start.3 = (bf16[1024,640]{1,0:T(8,128)(2,1)}, bf16[1024,640]{1,0:T(8,128)(2,1)}, u32[]{:S(2)}, u32[]{:S(2)}) collective-permute-start(bf16[1024,640]{1,0:T(8,128)(2,1)} %get-tuple-element.15), channel_id=1, source_target_pairs={{0,1},{1,0},{2,3},{3,2},{4,5},{5,4},{6,7},{7,6},{8,9},{9,8},{10,11... | collective-permute-start | bytes 3932168 | tf_op jit(solution)/shard_map/ppermute | solution.py:280
  105.4 2.2 %copy-start.5 = (bf16[1024,1280]{1,0:T(8,128)(2,1)S(1)}, bf16[1024,1280]{1,0:T(8,128)(2,1)}, u32[]{:S(2)}) copy-start(bf16[1024,1280]{1,0:T(8,128)(2,1)} %get-tuple-element.14) | copy-start | bytes 7864324
  109.2 1.5 %copy-start.6 = (bf16[1,1024,1280]{2,1,0:T(8,128)(2,1)}, bf16[1,1024,1280]{2,1,0:T(8,128)(2,1)S(1)}, u32[]{:S(2)}) copy-start(bf16[1,1024,1280]{2,1,0:T(8,128)(2,1)S(1)} %bitcast_dynamic-update-slice_fusion) | copy-start | bytes 7864324
